TPU v7x, 32 devices: a whole 2x2x4 slice. The times are simulated.
32 devices in a mesh: row: 4 (over y, x), query: 8 (over z, core).
Axes of the slice: x: 2, y: 2, z: 4, core: 2. Of those that a mesh axis runs over, the one named last changes fastest.
Arguments:
- logits: float32 [512, 1024], P('row'), may hold values from -9 to 309
- attributes: int32 [3, 16384], P(None, 'query'), may hold values from 0 to 63
- values: int32 [3, 16384], P(None, 'query'), may hold values from 0 to 15
- targets: float32 [16384], P('query'), may hold values from 0.25 to 1.75
Outputs:
- new_rows: float32 [512, 1024], P('row')
- residual: float32 [16384], P('query')
All inputs are finite; a program needn't handle non-finite values.
Results may differ from a plain program's by a relative error of at most 0.0064.
Values sent between devices are 32-bit elements; how exact they have to be, the bound alone decides.
A program may use at most 64 MiB of HBM per device.

v0:
```python
import jax
import jax.numpy as jnp
from jax import lax
from jax.sharding import PartitionSpec as P

VALS = 16
STEP_RATE = 2.0


def group_softmax(logit_rows):
    row_count = logit_rows.shape[0]
    grouped = logit_rows.reshape(row_count, -1, VALS)
    return jax.nn.softmax(grouped, axis=-1).reshape(row_count, -1)


def relaxed_update(logit_rows, relaxed, accumulated):
    row_count = logit_rows.shape[0]
    scaled = float(VALS * VALS) * accumulated
    grouped_p = relaxed.reshape(row_count, -1, VALS)
    grouped_d = scaled.reshape(row_count, -1, VALS)
    weighted_mean = jnp.sum(grouped_p * grouped_d, axis=-1, keepdims=True)
    tangent = (grouped_p * (grouped_d - weighted_mean)).reshape(row_count, -1)
    return group_softmax(logit_rows - STEP_RATE * tangent)


def make_selectors(columns, col_width):
    col_positions = jnp.arange(col_width, dtype=jnp.int32)[:, None]
    return [
        (col_positions == columns[slot_index][None, :]).astype(jnp.bfloat16)
        for slot_index in range(3)
    ]


def pick_columns(relaxed_b, selectors):
    return [
        jnp.dot(relaxed_b, selector, preferred_element_type=jnp.float32) for selector in selectors
    ]


def weight_sums(picked, misfit, selectors, running):
    weights = [
        (picked[1] * picked[2] * misfit).astype(jnp.bfloat16),
        (picked[0] * picked[2] * misfit).astype(jnp.bfloat16),
        (picked[0] * picked[1] * misfit).astype(jnp.bfloat16),
    ]
    for slot_index in range(3):
        running = running + lax.dot_general(
            weights[slot_index],
            selectors[slot_index],
            (((1,), (1,)), ((), ())),
            preferred_element_type=jnp.float32,
        )
    return running


def local(logits, attributes, values, targets):
    row_count, col_width = logits.shape
    total_rows = row_count * lax.axis_size("row")
    answer_scale = float(VALS**3) / total_rows
    relaxed = group_softmax(logits)
    relaxed_b = relaxed.astype(jnp.bfloat16)
    columns = attributes * VALS + values
    selectors = make_selectors(columns, col_width)
    picked = pick_columns(relaxed_b, selectors)
    partial_answers = jnp.sum(picked[0] * picked[1] * picked[2], axis=0)
    answers = lax.psum(partial_answers, "row") * answer_scale
    residual = answers - targets
    accumulated = weight_sums(
        picked, residual[None, :], selectors, jnp.zeros((row_count, col_width), jnp.float32)
    )
    share = lax.psum_scatter(accumulated, "query", scatter_dimension=1, tiled=True)
    share_width = share.shape[1]
    share_start = lax.axis_index("query") * share_width
    logit_share = lax.dynamic_slice_in_dim(logits, share_start, share_width, 1)
    relaxed_share = lax.dynamic_slice_in_dim(relaxed, share_start, share_width, 1)
    updated_share = relaxed_update(logit_share, relaxed_share, share)
    new_rows = lax.all_gather(updated_share, "query", axis=1, tiled=True)
    return (new_rows, residual)


def solution(mesh):
    placed = (P("row", None), P(None, "query"), P(None, "query"), P("query"))
    return jax.shard_map(
        local, mesh=mesh, in_specs=placed, out_specs=(P("row", None), P("query")), check_vma=False
    )
```

profile of v0, /device:TPU:0, one launch (start us, length us, event | category | flops | bytes accessed | tf_op | source)
XLA Modules:
  0.0 93.2 jit_solution(4023043113153630914)
XLA Ops:
  7.2 0.0 reduce-scatter.2.cloned.1.call-start
  7.2 1.2 %copy.6 = f32[128,1024]{0,1:T(8,128)S(1)} copy(f32[128,1024]{1,0:T(8,128)} %param.4) | data formatting | bytes 1048576 | tf_op args[0]
  8.4 0.1 bitcast_reduce_fusion
  8.5 1.5 %fusion.2 = f32[128,64,16]{0,2,1:T(8,128)S(1)} fusion(f32[128,1024]{0,1:T(8,128)S(1)} %copy.6, f32[128,64]{0,1:T(8,128)S(1)} %bitcast_reduce_fusion), kind=kOutput, calls=%fused_computation.2 | output fusion | flops 139279 | bytes 1081344 | tf_op jit(solution)/shard_map/div | solution.py:13
  10.0 0.2 copy.8
  10.2 0.0 copy-start.3
  10.2 0.0 copy-start.4
  10.3 0.0 copy-start
  10.3 0.2 copy.7
  10.5 0.5 copy-done.3
  11.0 0.0 copy-done.4
  11.1 0.3 copy-done
  11.3 0.2 exponential_divide_fusion
  11.5 1.8 %fusion.8 = f32[128,2048]{1,0:T(8,128)S(1)} fusion(s32[2048]{0:T(1024)S(1)} %bitcast.35, f32[128,1024]{1,0:T(8,128)S(1)} %exponential_divide_fusion), kind=kOutput, calls=%fused_computation.11 | convolution fusion | flops 539099136 | bytes 1581056 | tf_op jit(solution)/shard_map/dot_general | solution.py:36
  13.3 0.0 copy-start.1
  13.3 1.8 %fusion.4 = f32[128,2048]{1,0:T(8,128)S(1)} fusion(s32[2048]{0:T(1024)S(1)} %bitcast.37, f32[128,1024]{1,0:T(8,128)S(1)} %exponential_divide_fusion), kind=kOutput, calls=%fused_computation.5 | convolution fusion | flops 539099136 | bytes 1581056 | tf_op jit(solution)/shard_map/dot_general | solution.py:36
  15.1 0.0 copy-done.1
  15.1 0.0 copy-start.5
  15.1 2.8 %multiply_reduce_fusion = (f32[2048]{0:T(1024)S(1)}, f32[128,2048]{1,0:T(8,128)}, f32[128,2048]{1,0:T(8,128)S(1)}) fusion(f32[128,2048]{1,0:T(8,128)S(1)} %fusion.4, f32[128,2048]{1,0:T(8,128)S(1)} %fusion.8, s32[2048]{0:T(1024)S(1)} %bitcast.33, f32[128,1024]{1,0:T(8,128)S(1)} %exponential_divide_fusion), kind=kOutput, calls=%fused_computation.23 | convolution fusion | flops 539883520 | bytes 4734976 | tf_op jit(solution)/shard_map/dot_general | solution.py:36
  17.9 11.5 %psum.7 = f32[2048]{0:T(1024)S(1)} all-reduce(f32[2048]{0:T(1024)S(1)} %get-tuple-element.2), channel_id=1, replica_groups=mesh['row'=4,'query'=8] {'row'}, use_global_device_ids=true, to_apply=%region_3.0 | all-reduce | flops 2048 | bytes 16384 | tf_op jit(solution)/shard_map/psum | solution.py:66
  29.4 0.0 copy-done.5
  29.5 0.0 copy-start.6
  29.5 0.0 copy-start.2
  29.5 3.2 %fusion.3 = f32[128,1024]{1,0:T(8,128)S(1)} fusion(s32[2048]{0:T(1024)S(1)} %bitcast.38, f32[128,2048]{1,0:T(8,128)} %copy-done.1, f32[128,2048]{1,0:T(8,128)S(1)} %get-tuple-element.7, f32[2048]{0:T(1024)S(1)} %multiply_subtract_fusion.1), kind=kOutput, calls=%fused_computation.4 | convolution fusion | flops 539754496 | bytes 2637824 | tf_op jit(solution)/shard_map/dot_general | solution.py:47
  32.7 0.0 copy-done.2
  32.7 1.9 %fusion.5 = f32[128,1024]{1,0:T(8,128)S(1)} fusion(s32[2048]{0:T(1024)S(1)} %bitcast.34, f32[128,2048]{1,0:T(8,128)S(1)} %copy-done.2, f32[2048]{0:T(1024)S(1)} %multiply_subtract_fusion.1), kind=kOutput, calls=%fused_computation.7 | convolution fusion | flops 539492352 | bytes 1589248 | tf_op jit(solution)/shard_map/dot_general | solution.py:47
  34.6 0.0 copy-done.6
  34.6 2.7 %fusion.16 = f32[128,1024]{1,0:T(8,128)} fusion(f32[128,1024]{1,0:T(8,128)S(1)} %fusion.5, f32[128,1024]{1,0:T(8,128)S(1)} %fusion.3, s32[2048]{0:T(1024)S(1)} %bitcast.36, f32[128,2048]{1,0:T(8,128)S(1)} %fusion.4, f32[128,2048]{1,0:T(8,128)S(1)} %get-tuple-element.7, f32[2048]{0:T(1024)S(1)} %multiply_subtract_fusion.1), kind=kOutput, calls=%fused_computation.19 | convolution fusion | flops 540016640 | bytes 3686400 | tf_op jit(solution)/shard_map/dot_general | solution.py:47
  37.3 0.0 reduce-scatter.2.cloned.1.call-update
  37.4 30.5 %reduce-scatter.2.cloned.1.call-done = f32[128,128]{1,0:T(8,128)} async-done(((f32[128,1024]{1,0:T(8,128)}), f32[128,128]{1,0:T(8,128)}) %reduce-scatter.2.cloned.1.call-update) | async-done | bytes 65552 | tf_op jit(solution)/shard_map/reduce_scatter | solution.py:71
  67.9 0.9 multiply_multiply_fusion
  68.7 0.1 copy.9
  68.8 0.2 fusion.1
  69.0 0.1 copy.10
  69.1 0.9 multiply_subtract_fusion
  69.9 0.1 copy.11
  70.1 0.2 fusion
  70.3 0.1 copy.12
  70.4 0.1 copy.13
  70.5 15.0 %all_gather.3 = f32[128,1024]{1,0:T(8,128)S(1)} all-gather(f32[128,128]{1,0:T(8,128)S(1)} %exponential_divide_fusion.1), channel_id=1, replica_groups=mesh['row'=4,'query'=8] {'query'}, dimensions={1}, use_global_device_ids=true | all-gather | bytes 589824 | tf_op jit(solution)/shard_map/all_gather | solution.py:77
  85.5 0.8 copy.15
  (7 shorter events, 0.1 us)
Async XLA Ops:
  7.2 60.7 %reduce-scatter.2.cloned.1.call-start = ((), (), s32[]{:S(2)}) async-start(), calls=%async_computation.1 | async-start | bytes 589824 | tf_op jit(solution)/shard_map/reduce_scatter | solution.py:71
  10.2 0.8 copy-start.3
  10.2 0.8 copy-start.4
  10.3 1.1 %copy-start = (f32[128,1024]{1,0:T(8,128)S(1)}, f32[128,1024]{1,0:T(8,128)}, u32[]{:S(2)}) copy-start(f32[128,1024]{1,0:T(8,128)} %param.4) | copy-start | bytes 1572868
  13.3 1.8 %copy-start.1 = (f32[128,2048]{1,0:T(8,128)}, f32[128,2048]{1,0:T(8,128)S(1)}, u32[]{:S(2)}) copy-start(f32[128,2048]{1,0:T(8,128)S(1)} %fusion.8) | copy-start | bytes 3145732
  15.1 14.3 %copy-start.5 = (f32[2048]{0:T(1024)S(1)}, f32[2048]{0:T(1024)}, u32[]{:S(2)}) copy-start(f32[2048]{0:T(1024)} %param.7) | copy-start | bytes 24580
  29.5 5.1 %copy-start.6 = (f32[2048]{0:T(1024)}, f32[2048]{0:T(1024)S(1)}, u32[]{:S(2)}) copy-start(f32[2048]{0:T(1024)S(1)} %multiply_subtract_fusion.1) | copy-start | bytes 24580
  29.5 3.2 %copy-start.2 = (f32[128,2048]{1,0:T(8,128)S(1)}, f32[128,2048]{1,0:T(8,128)}, u32[]{:S(2)}) copy-start(f32[128,2048]{1,0:T(8,128)} %get-tuple-element.3) | copy-start | bytes 3145732
Sparse Core Ops, SparseCore 0:
  37.5 30.3 reduce-scatter.1
where the time goes:
time: 93.5 us; the launch traced here: 93.2 us
  waiting for transfers between devices  30.5 us (33%)
  blocking collectives  26.5 us (28%)
  between operations  14.3 us (15%)
  matrix products  14.2 us (15%)
  other arithmetic  3.85 us (4%)
  local copies, waits for them, and re-layouts  3.71 us (4%)
    reduce_scatter x1, waiting for transfers between devices, local(): lax.psum_scatter(accumulated, 'query', scatter_dimension=1, tiled=True)  30.5 us
    all_gather x1, blocking collectives, local(): new_rows = lax.all_gather(updated_share, 'query', axis=1, tiled=True)  15 us
    psum x1, blocking collectives, local(): answers = lax.psum(partial_answers, 'row') * answer_scale  11.5 us
    dot_general x3, matrix products, weight_sums(): lax.dot_general(weights[slot_index], selectors[slot_index], (((1,), (1,))...  7.81 us
    dot_general x3, matrix products, pick_columns(): jnp.dot(relaxed_b, selector, preferred_element_type=jnp.float32)  6.42 us
    unnamed x16, local copies, waits for them, and re-layouts  2.82 us
  transfers between devices with their start and end apart: 1, of which 1 were waited for; matrix products, arithmetic and copies ran while one was open for 0% of the time, Pallas kernels for 0%

commit v1 on v0

--- a/solution.py
+++ b/solution.py
@@ -5,6 +5,12 @@
 
 VALS = 16
 STEP_RATE = 2.0
+
+
+def laid_out(blocks, dim):
+    dims = list(blocks.shape[1:])
+    dims[dim] *= blocks.shape[0]
+    return jnp.moveaxis(blocks, 0, dim).reshape(dims)
 
 
 def group_softmax(logit_rows):
@@ -74,7 +80,19 @@
     logit_share = lax.dynamic_slice_in_dim(logits, share_start, share_width, 1)
     relaxed_share = lax.dynamic_slice_in_dim(relaxed, share_start, share_width, 1)
     updated_share = relaxed_update(logit_share, relaxed_share, share)
-    new_rows = lax.all_gather(updated_share, "query", axis=1, tiled=True)
+    peers = lax.axis_size("query")
+    pairs = [(i, (i + 1) % peers) for i in range(peers)]
+    back = [(b, a) for a, b in pairs]
+    lower, upper = ([], [])
+    for turn in range(peers - 1):
+        if turn % 2 == 0:
+            lower.append(lax.ppermute(lower[-1] if lower else updated_share, "query", pairs))
+        else:
+            upper.append(lax.ppermute(upper[-1] if upper else updated_share, "query", back))
+    tiles = jnp.stack([*lower[::-1], updated_share, *upper])
+    shift = lax.axis_index("query") - len(lower)
+    tiles = tiles[(jnp.arange(peers) - shift) % peers]
+    new_rows = laid_out(tiles, 1)
     return (new_rows, residual)
 
 

time: 93.5 us -> 102 us (1.091)
  blocking collectives: 26.5 us -> 11.5 us
  waiting for transfers between devices: 30.5 us -> 42 us
  starting transfers between devices: 0.04 us -> 10.8 us
  local copies, waits for them, and re-layouts: 3.71 us -> 4.75 us
    all_gather x1 -> x0, blocking collectives: 15 us -> none  [local(): new_rows = lax.all_gather(updated_share, 'query', axis=1, tiled=True)]
    ppermute x0 -> x7, waiting for transfers between devices: none -> 11.5 us  [the longest x4 11.4 us: local(): lax.ppermute(lower[-1] if lower else updated_share, 'query', pairs)]
    ppermute x0 -> x7, starting transfers between devices: none -> 10.8 us  [the longest x3 10.7 us: local(): lax.ppermute(upper[-1] if upper else updated_share, 'query', back)]
    unnamed x16 -> x23, local copies, waits for them, and re-layouts: 2.82 us -> 3.07 us
  transfers between devices with their start and end apart: 1 -> 8, of which waited for: 1 -> 5; matrix products, arithmetic and copies ran while one was open for 0% -> 0% of each run, Pallas kernels for 0% -> 0%
where the time goes in v1:
time: 102 us
  waiting for transfers between devices  42 us (41%)
  between operations  14.4 us (14%)
  matrix products  14.2 us (14%)
  blocking collectives  11.5 us (11%)
  starting transfers between devices  10.8 us (11%)
  local copies, waits for them, and re-layouts  4.75 us (5%)
  other arithmetic  3.87 us (4%)
    reduce_scatter x1, waiting for transfers between devices, local(): lax.psum_scatter(accumulated, 'query', scatter_dimension=1, tiled=True)  30.5 us
    psum x1, blocking collectives, local(): answers = lax.psum(partial_answers, 'row') * answer_scale  11.5 us
    ppermute x4, waiting for transfers between devices, local(): lax.ppermute(lower[-1] if lower else updated_share, 'query', pairs)  11.4 us
    ppermute x3, starting transfers between devices, local(): lax.ppermute(upper[-1] if upper else updated_share, 'query', back)  10.7 us
    dot_general x3, matrix products, weight_sums(): lax.dot_general(weights[slot_index], selectors[slot_index], (((1,), (1,))...  7.81 us
    dot_general x3, matrix products, pick_columns(): jnp.dot(relaxed_b, selector, preferred_element_type=jnp.float32)  6.42 us
    unnamed x23, local copies, waits for them, and re-layouts  3.07 us
  transfers between devices with their start and end apart: 8, of which 5 were waited for; matrix products, arithmetic and copies ran while one was open for 0% of the time, Pallas kernels for 0%

profile of v1, /device:TPU:0, one launch (start us, length us, event | category | flops | bytes accessed | tf_op | source)
XLA Modules:
  0.0 101.5 jit_solution(18396470967932403575)
XLA Ops:
  7.2 0.0 reduce-scatter.2.cloned.1.call-start
  7.2 1.2 %copy.6 = f32[128,1024]{0,1:T(8,128)S(1)} copy(f32[128,1024]{1,0:T(8,128)} %param.4) | data formatting | bytes 1048576 | tf_op args[0]
  8.4 0.1 bitcast_reduce_fusion
  8.5 1.5 %fusion.2 = f32[128,64,16]{0,2,1:T(8,128)S(1)} fusion(f32[128,1024]{0,1:T(8,128)S(1)} %copy.6, f32[128,64]{0,1:T(8,128)S(1)} %bitcast_reduce_fusion), kind=kOutput, calls=%fused_computation.3 | output fusion | flops 139279 | bytes 1081344 | tf_op jit(solution)/shard_map/div | solution.py:19
  10.0 0.2 copy.8
  10.2 0.0 copy-start.3
  10.2 0.0 copy-start.4
  10.3 0.0 copy-start
  10.3 0.2 copy.7
  10.5 0.5 copy-done.3
  11.0 0.0 copy-done.4
  11.1 0.3 copy-done
  11.3 0.2 exponential_divide_fusion
  11.5 1.8 %fusion.8 = f32[128,2048]{1,0:T(8,128)S(1)} fusion(s32[2048]{0:T(1024)S(1)} %bitcast.57, f32[128,1024]{1,0:T(8,128)S(1)} %exponential_divide_fusion), kind=kOutput, calls=%fused_computation.12 | convolution fusion | flops 539099136 | bytes 1581056 | tf_op jit(solution)/shard_map/dot_general | solution.py:42
  13.3 0.0 copy-start.1
  13.3 1.8 %fusion.4 = f32[128,2048]{1,0:T(8,128)S(1)} fusion(s32[2048]{0:T(1024)S(1)} %bitcast.59, f32[128,1024]{1,0:T(8,128)S(1)} %exponential_divide_fusion), kind=kOutput, calls=%fused_computation.6 | convolution fusion | flops 539099136 | bytes 1581056 | tf_op jit(solution)/shard_map/dot_general | solution.py:42
  15.1 0.0 copy-done.1
  15.1 0.0 copy-start.5
  15.1 2.8 %multiply_reduce_fusion = (f32[2048]{0:T(1024)S(1)}, f32[128,2048]{1,0:T(8,128)}, f32[128,2048]{1,0:T(8,128)S(1)}) fusion(f32[128,2048]{1,0:T(8,128)S(1)} %fusion.4, f32[128,2048]{1,0:T(8,128)S(1)} %fusion.8, s32[2048]{0:T(1024)S(1)} %bitcast.55, f32[128,1024]{1,0:T(8,128)S(1)} %exponential_divide_fusion), kind=kOutput, calls=%fused_computation.24 | convolution fusion | flops 539883520 | bytes 4734976 | tf_op jit(solution)/shard_map/dot_general | solution.py:42
  17.9 11.5 %psum.7 = f32[2048]{0:T(1024)S(1)} all-reduce(f32[2048]{0:T(1024)S(1)} %get-tuple-element.4), channel_id=1, replica_groups=mesh['row'=4,'query'=8] {'row'}, use_global_device_ids=true, to_apply=%region_3.0 | all-reduce | flops 2048 | bytes 16384 | tf_op jit(solution)/shard_map/psum | solution.py:72
  29.4 0.0 copy-done.5
  29.5 0.0 copy-start.6
  29.5 0.0 copy-start.2
  29.5 3.2 %fusion.3 = f32[128,1024]{1,0:T(8,128)S(1)} fusion(s32[2048]{0:T(1024)S(1)} %bitcast.60, f32[128,2048]{1,0:T(8,128)} %copy-done.1, f32[128,2048]{1,0:T(8,128)S(1)} %get-tuple-element.9, f32[2048]{0:T(1024)S(1)} %multiply_subtract_fusion.1), kind=kOutput, calls=%fused_computation.5 | convolution fusion | flops 539754496 | bytes 2637824 | tf_op jit(solution)/shard_map/dot_general | solution.py:53
  32.7 0.0 copy-done.2
  32.7 1.9 %fusion.5 = f32[128,1024]{1,0:T(8,128)S(1)} fusion(s32[2048]{0:T(1024)S(1)} %bitcast.56, f32[128,2048]{1,0:T(8,128)S(1)} %copy-done.2, f32[2048]{0:T(1024)S(1)} %multiply_subtract_fusion.1), kind=kOutput, calls=%fused_computation.8 | convolution fusion | flops 539492352 | bytes 1589248 | tf_op jit(solution)/shard_map/dot_general | solution.py:53
  34.6 0.0 copy-done.6
  34.6 2.7 %fusion.16 = f32[128,1024]{1,0:T(8,128)} fusion(f32[128,1024]{1,0:T(8,128)S(1)} %fusion.5, f32[128,1024]{1,0:T(8,128)S(1)} %fusion.3, s32[2048]{0:T(1024)S(1)} %bitcast.58, f32[128,2048]{1,0:T(8,128)S(1)} %fusion.4, f32[128,2048]{1,0:T(8,128)S(1)} %get-tuple-element.9, f32[2048]{0:T(1024)S(1)} %multiply_subtract_fusion.1), kind=kOutput, calls=%fused_computation.20 | convolution fusion | flops 540016640 | bytes 3686400 | tf_op jit(solution)/shard_map/dot_general | solution.py:53
  37.3 0.0 reduce-scatter.2.cloned.1.call-update
  37.4 30.5 %reduce-scatter.2.cloned.1.call-done = f32[128,128]{1,0:T(8,128)} async-done(((f32[128,1024]{1,0:T(8,128)}), f32[128,128]{1,0:T(8,128)}) %reduce-scatter.2.cloned.1.call-update) | async-done | bytes 65552 | tf_op jit(solution)/shard_map/reduce_scatter | solution.py:77
  67.9 0.9 multiply_multiply_fusion
  68.7 0.1 copy.9
  68.8 0.2 fusion.1
  69.0 0.1 copy.10
  69.1 0.9 multiply_subtract_fusion
  69.9 0.1 copy.11
  70.1 0.2 fusion
  70.3 0.1 copy.12
  70.4 0.1 copy.13
  70.5 0.1 collective-permute-start
  70.6 5.5 %collective-permute-done = f32[128,128]{1,0:T(8,128)S(1)} collective-permute-done((f32[128,128]{1,0:T(8,128)S(1)}, f32[128,128]{1,0:T(8,128)S(1)}, u32[]{:S(2)}, u32[]{:S(2)}) %collective-permute-start) | collective-permute-done | bytes 65568 | tf_op jit(solution)/shard_map/ppermute | solution.py:89
  76.1 0.0 collective-permute-start.1
  76.1 3.5 %collective-permute-start.4 = (f32[128,128]{1,0:T(8,128)S(1)}, f32[128,128]{1,0:T(8,128)S(1)}, u32[]{:S(2)}, u32[]{:S(2)}) collective-permute-start(f32[128,128]{1,0:T(8,128)S(1)} %exponential_divide_fusion.1), channel_id=1, source_target_pairs={{1,0},{2,1},{3,2},{4,3},{5,4},{6,5},{7,6},{0,7},{9,8},{10,9},{11,1... | collective-permute-start | bytes 196616 | tf_op jit(solution)/shard_map/ppermute | solution.py:91
  79.7 2.0 %collective-permute-done.1 = f32[128,128]{1,0:T(8,128)S(1)} collective-permute-done((f32[128,128]{1,0:T(8,128)S(1)}, f32[128,128]{1,0:T(8,128)S(1)}, u32[]{:S(2)}, u32[]{:S(2)}) %collective-permute-start.1) | collective-permute-done | bytes 65568 | tf_op jit(solution)/shard_map/ppermute | solution.py:89
  81.7 0.0 collective-permute-start.2
  81.7 0.0 collective-permute-done.4
  81.7 3.6 %collective-permute-start.5 = (f32[128,128]{1,0:T(8,128)S(1)}, f32[128,128]{1,0:T(8,128)S(1)}, u32[]{:S(2)}, u32[]{:S(2)}) collective-permute-start(f32[128,128]{1,0:T(8,128)S(1)} %collective-permute-done.4), channel_id=1, source_target_pairs={{1,0},{2,1},{3,2},{4,3},{5,4},{6,5},{7,6},{0,7},{9,8},{10,9},{11,1... | collective-permute-start | bytes 196616 | tf_op jit(solution)/shard_map/ppermute | solution.py:91
  85.3 2.0 %collective-permute-done.2 = f32[128,128]{1,0:T(8,128)S(1)} collective-permute-done((f32[128,128]{1,0:T(8,128)S(1)}, f32[128,128]{1,0:T(8,128)S(1)}, u32[]{:S(2)}, u32[]{:S(2)}) %collective-permute-start.2) | collective-permute-done | bytes 65568 | tf_op jit(solution)/shard_map/ppermute | solution.py:89
  87.3 0.0 collective-permute-start.3
  87.3 0.0 collective-permute-done.5
  87.3 3.6 %collective-permute-start.6 = (f32[128,128]{1,0:T(8,128)S(1)}, f32[128,128]{1,0:T(8,128)S(1)}, u32[]{:S(2)}, u32[]{:S(2)}) collective-permute-start(f32[128,128]{1,0:T(8,128)S(1)} %collective-permute-done.5), channel_id=1, source_target_pairs={{1,0},{2,1},{3,2},{4,3},{5,4},{6,5},{7,6},{0,7},{9,8},{10,9},{11,1... | collective-permute-start | bytes 196616 | tf_op jit(solution)/shard_map/ppermute | solution.py:91
  90.9 1.9 %collective-permute-done.3 = f32[128,128]{1,0:T(8,128)S(1)} collective-permute-done((f32[128,128]{1,0:T(8,128)S(1)}, f32[128,128]{1,0:T(8,128)S(1)}, u32[]{:S(2)}, u32[]{:S(2)}) %collective-permute-start.3) | collective-permute-done | bytes 65568 | tf_op jit(solution)/shard_map/ppermute | solution.py:89
  92.9 0.0 collective-permute-done.6
  92.9 0.6 gather_fusion
  93.5 0.2 copy.14
  93.7 1.0 copy.15
  (17 shorter events, 0.2 us)
Async XLA Ops:
  7.2 60.7 %reduce-scatter.2.cloned.1.call-start = ((), (), s32[]{:S(2)}) async-start(), calls=%async_computation.1 | async-start | bytes 589824 | tf_op jit(solution)/shard_map/reduce_scatter | solution.py:77
  10.2 0.8 copy-start.3
  10.2 0.8 copy-start.4
  10.3 1.1 %copy-start = (f32[128,1024]{1,0:T(8,128)S(1)}, f32[128,1024]{1,0:T(8,128)}, u32[]{:S(2)}) copy-start(f32[128,1024]{1,0:T(8,128)} %param.4) | copy-start | bytes 1572868
  13.3 1.8 %copy-start.1 = (f32[128,2048]{1,0:T(8,128)}, f32[128,2048]{1,0:T(8,128)S(1)}, u32[]{:S(2)}) copy-start(f32[128,2048]{1,0:T(8,128)S(1)} %fusion.8) | copy-start | bytes 3145732
  15.1 14.3 %copy-start.5 = (f32[2048]{0:T(1024)S(1)}, f32[2048]{0:T(1024)}, u32[]{:S(2)}) copy-start(f32[2048]{0:T(1024)} %param.7) | copy-start | bytes 24580
  29.5 5.1 %copy-start.6 = (f32[2048]{0:T(1024)}, f32[2048]{0:T(1024)S(1)}, u32[]{:S(2)}) copy-start(f32[2048]{0:T(1024)S(1)} %multiply_subtract_fusion.1) | copy-start | bytes 24580
  29.5 3.2 %copy-start.2 = (f32[128,2048]{1,0:T(8,128)S(1)}, f32[128,2048]{1,0:T(8,128)}, u32[]{:S(2)}) copy-start(f32[128,2048]{1,0:T(8,128)} %get-tuple-element.5) | copy-start | bytes 3145732
  70.5 5.6 %collective-permute-start = (f32[128,128]{1,0:T(8,128)S(1)}, f32[128,128]{1,0:T(8,128)S(1)}, u32[]{:S(2)}, u32[]{:S(2)}) collective-permute-start(f32[128,128]{1,0:T(8,128)S(1)} %exponential_divide_fusion.1), channel_id=1, source_target_pairs={{0,1},{1,2},{2,3},{3,4},{4,5},{5,6},{6,7},{7,0},{8,9},{9,10},{10,1... | collective-permute-start | bytes 196616 | tf_op jit(solution)/shard_map/ppermute | solution.py:89
  76.1 5.6 %collective-permute-start.1 = (f32[128,128]{1,0:T(8,128)S(1)}, f32[128,128]{1,0:T(8,128)S(1)}, u32[]{:S(2)}, u32[]{:S(2)}) collective-permute-start(f32[128,128]{1,0:T(8,128)S(1)} %collective-permute-done), channel_id=1, source_target_pairs={{0,1},{1,2},{2,3},{3,4},{4,5},{5,6},{6,7},{7,0},{8,9},{9,10},{10,1... | collective-permute-start | bytes 196616 | tf_op jit(solution)/shard_map/ppermute | solution.py:89
  76.1 5.6 %collective-permute-start.4 = (f32[128,128]{1,0:T(8,128)S(1)}, f32[128,128]{1,0:T(8,128)S(1)}, u32[]{:S(2)}, u32[]{:S(2)}) collective-permute-start(f32[128,128]{1,0:T(8,128)S(1)} %exponential_divide_fusion.1), channel_id=1, source_target_pairs={{1,0},{2,1},{3,2},{4,3},{5,4},{6,5},{7,6},{0,7},{9,8},{10,9},{11,1... | collective-permute-start | bytes 196616 | tf_op jit(solution)/shard_map/ppermute | solution.py:91
  81.7 5.6 %collective-permute-start.2 = (f32[128,128]{1,0:T(8,128)S(1)}, f32[128,128]{1,0:T(8,128)S(1)}, u32[]{:S(2)}, u32[]{:S(2)}) collective-permute-start(f32[128,128]{1,0:T(8,128)S(1)} %collective-permute-done.1), channel_id=1, source_target_pairs={{0,1},{1,2},{2,3},{3,4},{4,5},{5,6},{6,7},{7,0},{8,9},{9,10},{10,1... | collective-permute-start | bytes 196616 | tf_op jit(solution)/shard_map/ppermute | solution.py:89
  81.7 5.6 %collective-permute-start.5 = (f32[128,128]{1,0:T(8,128)S(1)}, f32[128,128]{1,0:T(8,128)S(1)}, u32[]{:S(2)}, u32[]{:S(2)}) collective-permute-start(f32[128,128]{1,0:T(8,128)S(1)} %collective-permute-done.4), channel_id=1, source_target_pairs={{1,0},{2,1},{3,2},{4,3},{5,4},{6,5},{7,6},{0,7},{9,8},{10,9},{11,1... | collective-permute-start | bytes 196616 | tf_op jit(solution)/shard_map/ppermute | solution.py:91
  87.3 5.5 %collective-permute-start.3 = (f32[128,128]{1,0:T(8,128)S(1)}, f32[128,128]{1,0:T(8,128)S(1)}, u32[]{:S(2)}, u32[]{:S(2)}) collective-permute-start(f32[128,128]{1,0:T(8,128)S(1)} %collective-permute-done.2), channel_id=1, source_target_pairs={{0,1},{1,2},{2,3},{3,4},{4,5},{5,6},{6,7},{7,0},{8,9},{9,10},{10,1... | collective-permute-start | bytes 196616 | tf_op jit(solution)/shard_map/ppermute | solution.py:89
  87.3 5.6 %collective-permute-start.6 = (f32[128,128]{1,0:T(8,128)S(1)}, f32[128,128]{1,0:T(8,128)S(1)}, u32[]{:S(2)}, u32[]{:S(2)}) collective-permute-start(f32[128,128]{1,0:T(8,128)S(1)} %collective-permute-done.5), channel_id=1, source_target_pairs={{1,0},{2,1},{3,2},{4,3},{5,4},{6,5},{7,6},{0,7},{9,8},{10,9},{11,1... | collective-permute-start | bytes 196616 | tf_op jit(solution)/shard_map/ppermute | solution.py:91
Sparse Core Ops, SparseCore 0:
  37.5 30.3 reduce-scatter.1
